TPU v7x, 512 devices: a whole 4x8x8 slice. The times are simulated.
512 devices in a mesh: blk: 8 (over y_lo, core), leaf: 64 (over z, y_hi, x).
Axes of the slice: x: 4, y: 8 (y_hi: 2, y_lo: 4; y = y_hi * 4 + y_lo), z: 8, core: 2. Of those that a mesh axis runs over, the one named last changes fastest.
Arguments:
- positions: float32 [3, 64, 8, 128], P(None, 'leaf', 'blk'), may hold values from 0 to 32, as said below
- panel_areas: float32 [64, 8, 128], P('leaf', 'blk'), may hold values from 0.5 to 2
- probe_cols: bfloat16 [576, 64, 8, 128], P(None, 'leaf', 'blk'), may hold values from -5 to 5
- full_sketch: bfloat16 [576, 64, 8, 128], P(None, 'leaf', 'blk'), may hold values from -3 to 3
- tree_order: int32 [64, 8, 128], P('leaf', 'blk'), may hold values from 0 to 127, each once within a row
- leaf_basis: bfloat16 [64, 8, 128, 512], P('leaf', 'blk'), may hold values from -0.1875 to 0.1875
- transfer_mats: bfloat16 [64, 3, 512, 512], P('leaf'), may hold values from -0.1875 to 0.1875
Outputs:
- offdiag_sketch: bfloat16 [576, 64, 8, 128], P(None, 'leaf', 'blk')
- nested_sketch: float32 [64, 2, 576, 512], P('leaf')
Inputs may be any that keep to these rules, and one draw needn't show every extreme that they name: `positions`: each leaf's panel centres lie on a surface patch of 32 by 32 mean panel widths. `tree_order`: along the last dimension, each row names every one of the 128 panels of its block once.
All inputs are finite; a program needn't handle non-finite values.
Results may differ from a plain program's by a relative error of at most 0.0046.
Values sent between devices are 32-bit elements; how exact they have to be, the bound alone decides.
No kernel may reach another device: no remote copies, remote signals or barrier semaphores. Data moves between devices by JAX's collectives and lax.ppermute only.
A program may use at most 64 MiB of HBM per device.

v0:
```python
import math
import jax
import jax.numpy as jnp
from jax import lax
from jax.sharding import PartitionSpec as P

inv_four_pi = 1.0 / (4.0 * math.pi)


def partner(value, axis, bit):
    mask = 2**bit
    pairs = [(source, source ^ mask) for source in range(lax.axis_size(axis))]
    return lax.ppermute(value, axis, pairs)


def kernel_tile(target_pos, target_area, source_pos, source_area):
    distance = jnp.zeros((target_pos.shape[1], source_pos.shape[1]), jnp.float32)
    for component in range(3):
        gap = target_pos[component][:, None] - source_pos[component][None, :]
        distance = distance + gap * gap
    soft = distance + 0.5 * (target_area[:, None] + source_area[None, :])
    return (inv_four_pi * lax.rsqrt(soft)).astype(jnp.bfloat16)


def target_blocks(target_pos, target_area):
    panels = target_pos.shape[1]
    block_size = min(512, panels)
    block_count = panels // block_size
    pos_blocks = jnp.transpose(target_pos.reshape(3, block_count, block_size), (1, 0, 2))
    return (pos_blocks, target_area.reshape(block_count, block_size))


def near_block(target_pos, target_area, source_pos, source_area, source_scaled):
    pos_blocks, area_blocks = target_blocks(target_pos, target_area)

    def one_block(entry):
        block_pos, block_area = entry
        kernel = kernel_tile(block_pos, block_area, source_pos, source_area)
        return lax.dot_general(
            source_scaled, kernel, (((1,), (1,)), ((), ())), preferred_element_type=jnp.float32
        )

    sums = lax.map(one_block, (pos_blocks, area_blocks))
    return jnp.transpose(sums, (1, 0, 2)).reshape(source_scaled.shape[0], target_pos.shape[1])


def project(current, level_mat):
    return jnp.dot(current, level_mat.astype(jnp.float32), precision=lax.Precision.HIGHEST)


def climb_rows(rows, level_mats):
    for tree_level in range(level_mats.shape[0]):
        projected = project(rows, level_mats[tree_level])
        rows = projected + partner(projected, "leaf", tree_level)
    return rows


def shards(positions, panel_areas, probe_cols, full_sketch, tree_order, leaf_basis, transfer_mats):
    panels = positions.shape[3]
    probe_count = probe_cols.shape[0]
    basis_width = leaf_basis.shape[3]
    level_count = transfer_mats.shape[1]
    coords = positions.reshape(3, panels)
    area_row = panel_areas.reshape(1, panels)
    probe_flat = probe_cols.reshape(probe_count, panels)
    scaled = (area_row * probe_flat.astype(jnp.float32)).astype(jnp.bfloat16)
    sorting = tree_order.reshape(panels)
    basis_flat = leaf_basis.reshape(panels, basis_width)
    level_mats = transfer_mats.reshape(level_count, basis_width, basis_width)
    probe_part = jnp.dot(
        jnp.take(probe_flat, sorting, axis=1), basis_flat, preferred_element_type=jnp.float32
    )
    outgoing = jnp.concatenate([coords, area_row, scaled.astype(jnp.float32)], axis=0)
    piece = lax.all_gather(outgoing, "ylo", axis=1, tiled=True)
    piece = lax.all_gather(piece, "core", axis=1, tiled=True)
    near_sum = near_block(coords, area_row[0], piece[:3], piece[3], piece[4:].astype(jnp.bfloat16))
    offdiag = (full_sketch.reshape(probe_count, panels).astype(jnp.float32) - near_sum).astype(
        jnp.bfloat16
    )
    sketch_part = jnp.dot(
        jnp.take(offdiag, sorting, axis=1), basis_flat, preferred_element_type=jnp.float32
    )
    stacked = jnp.concatenate([sketch_part, probe_part], axis=0)
    mine = lax.psum_scatter(stacked, "core", scatter_dimension=0, tiled=True)
    mine = lax.psum_scatter(mine, "ylo", scatter_dimension=0, tiled=True)
    top = climb_rows(mine, level_mats)
    top = lax.all_gather(top, "ylo", axis=0, tiled=True)
    nested = lax.all_gather(top, "core", axis=0, tiled=True).reshape(2, probe_count, basis_width)[
        None
    ]
    return (offdiag.reshape(probe_count, 1, 1, panels), nested)


def solution(mesh):
    blk = mesh.shape["blk"]
    devices = mesh.devices.reshape(blk // 2, 2, mesh.shape["leaf"])
    split_mesh = jax.sharding.Mesh(devices, ("ylo", "core", "leaf"))
    blk_axes = ("ylo", "core")
    in_specs = (
        P(None, "leaf", blk_axes, None),
        P("leaf", blk_axes, None),
        P(None, "leaf", blk_axes, None),
        P(None, "leaf", blk_axes, None),
        P("leaf", blk_axes, None),
        P("leaf", blk_axes, None, None),
        P("leaf", None, None, None),
    )
    out_specs = (P(None, "leaf", blk_axes, None), P("leaf", None, None, None))
    return jax.shard_map(
        shards, mesh=split_mesh, in_specs=in_specs, out_specs=out_specs, check_vma=False
    )
```

profile of v0, /device:TPU:1, one launch (start us, length us, event | category | flops | bytes accessed | tf_op | source)
XLA Modules:
  0.0 263.4 jit_solution(10981654303635103576)
XLA Ops:
  7.2 0.0 copy-start
  7.2 0.0 all-gather.5.cloned.1.call-start
  7.2 0.8 copy.15
  8.0 0.8 copy.13
  8.8 0.0 copy-start.5
  8.8 1.1 copy.14
  9.9 0.7 fusion.25
  10.6 0.9 pad_maximum_fusion.1
  11.5 0.0 copy-start.3
  11.5 0.0 all-gather.5.cloned.1.call-update
  11.6 0.0 all-gather.7.cloned.1.call-start
  11.6 45.6 %all-gather.5.cloned.1.call-done = f32[580,512]{0,1:T(8,128)} async-done(((f32[580,128]{0,1:T(8,128)}), f32[580,512]{0,1:T(8,128)}) %all-gather.5.cloned.1.call-update) | async-done | bytes 1187856 | tf_op jit(solution)/shard_map/all_gather | solution.py:74
  57.2 0.0 all-gather.7.cloned.1.call-update
  57.2 0.0 reduce-scatter.3.cloned.1.call-start
  57.3 0.0 copy-done.5
  57.3 0.9 gather_fusion.1
  58.2 0.0 copy-done.3
  58.2 0.0 copy-done
  58.2 0.0 copy-start.2
  58.2 0.0 copy-start.4
  58.3 0.4 fusion.26
  58.7 21.1 %all-gather.7.cloned.1.call-done = f32[580,1024]{0,1:T(8,128)} async-done(((f32[580,512]{0,1:T(8,128)}), f32[580,1024]{0,1:T(8,128)}) %all-gather.7.cloned.1.call-update) | async-done | bytes 2375696 | tf_op jit(solution)/shard_map/all_gather | solution.py:75
  79.7 3.2 %slice_reduce_fusion.3 = (f32[1024]{0:T(1024)S(1)}, f32[1024]{0:T(1024)S(1)}, f32[1024]{0:T(1024)S(1)}, f32[1024]{0:T(1024)S(1)}) fusion(f32[580,1024]{0,1:T(8,128)} %all-gather.7.cloned.1.call-done), kind=kLoop, calls=%fused_computation.8 | loop fusion | bytes 32768 | tf_op jit(solution)/shard_map/while/body/eval_jaxpr/slice | solution.py:19
  82.9 0.0 copy-done.2
  82.9 0.0 copy-done.4
  82.9 3.6 %fusion.10 = (bf16[576,1,1,128]{3,0,2,1:T(8,128)(2,1)}, f32[576,128]{1,0:T(8,128)S(1)}) fusion(bf16[576,1,1,128]{3,0,2,1:T(8,128)(2,1)S(1)} %copy-done.2, f32[1024]{0:T(1024)S(1)} %get-tuple-element.18, f32[128]{0:T(128)S(1)} %bitcast.50, f32[1024]{0:T(1024)S(1)} %get-tuple-element.19, f32[128]{0:T(128)S(1)} %get-tuple-element.29, ...), kind=kOutput, calls=%fused_computation.23 | convolution fusion | flops 152920064 | bytes 1918976 | tf_op jit(solution)/shard_map/while/body/eval_jaxpr/dot_general | solution.py:39
  86.5 0.2 copy.16
  86.7 0.9 gather_fusion
  87.6 0.4 fusion.28
  88.0 1.6 pad_maximum_fusion
  89.6 0.0 copy-start.1
  89.6 0.0 reduce-scatter.3.cloned.1.call-update
  89.6 0.0 reduce-scatter.5.cloned.1.call-start
  89.7 19.3 %reduce-scatter.3.cloned.1.call-done = f32[576,512]{1,0:T(8,128)} async-done(((f32[1152,512]{1,0:T(8,128)}), f32[576,512]{1,0:T(8,128)}) %reduce-scatter.3.cloned.1.call-update) | async-done | bytes 1179664 | tf_op jit(solution)/shard_map/reduce_scatter | solution.py:84
  108.9 0.0 reduce-scatter.5.cloned.1.call-update
  109.0 0.0 all-gather.9.cloned.1.call-start
  109.0 39.9 %reduce-scatter.5.cloned.1.call-done = f32[144,512]{1,0:T(8,128)} async-done(((f32[576,512]{1,0:T(8,128)}), f32[144,512]{1,0:T(8,128)}) %reduce-scatter.5.cloned.1.call-update) | async-done | bytes 294928 | tf_op jit(solution)/shard_map/reduce_scatter | solution.py:85
  148.9 0.0 copy-done.1
  148.9 1.4 fusion.5
  150.2 3.1 %collective-permute-start = (f32[144,512]{1,0:T(8,128)S(1)}, f32[144,512]{1,0:T(8,128)S(1)}, u32[]{:S(2)}, u32[]{:S(2)}) collective-permute-start(f32[144,512]{1,0:T(8,128)S(1)} %fusion.5), channel_id=1, source_target_pairs={{0,1},{1,0},{2,3},{3,2},{4,5},{5,4},{6,7},{7,6},{8,9},{9,8},{10,11... | collective-permute-start | bytes 884744 | tf_op jit(solution)/shard_map/ppermute | solution.py:13
  153.3 6.5 %collective-permute-done = f32[144,512]{1,0:T(8,128)S(1)} collective-permute-done((f32[144,512]{1,0:T(8,128)S(1)}, f32[144,512]{1,0:T(8,128)S(1)}, u32[]{:S(2)}, u32[]{:S(2)}) %collective-permute-start) | collective-permute-done | bytes 294944 | tf_op jit(solution)/shard_map/ppermute | solution.py:13
  159.8 0.4 fusion.3
  160.2 4.6 %collective-permute-start.1 = (f32[144,512]{1,0:T(8,128)S(1)}, f32[144,512]{1,0:T(8,128)S(1)}, u32[]{:S(2)}, u32[]{:S(2)}) collective-permute-start(f32[144,512]{1,0:T(8,128)S(1)} %fusion.3), channel_id=1, source_target_pairs={{0,2},{1,3},{2,0},{3,1},{4,6},{5,7},{6,4},{7,5},{8,10},{9,11},{10,... | collective-permute-start | bytes 884744 | tf_op jit(solution)/shard_map/ppermute | solution.py:13
  164.9 5.6 %collective-permute-done.1 = f32[144,512]{1,0:T(8,128)S(1)} collective-permute-done((f32[144,512]{1,0:T(8,128)S(1)}, f32[144,512]{1,0:T(8,128)S(1)}, u32[]{:S(2)}, u32[]{:S(2)}) %collective-permute-start.1) | collective-permute-done | bytes 294944 | tf_op jit(solution)/shard_map/ppermute | solution.py:13
  170.4 0.4 fusion.1
  170.8 6.3 %collective-permute-start.2 = (f32[144,512]{1,0:T(8,128)S(1)}, f32[144,512]{1,0:T(8,128)S(1)}, u32[]{:S(2)}, u32[]{:S(2)}) collective-permute-start(f32[144,512]{1,0:T(8,128)S(1)} %fusion.1), channel_id=1, source_target_pairs={{0,4},{1,5},{2,6},{3,7},{4,0},{5,1},{6,2},{7,3},{8,12},{9,13},{10,... | collective-permute-start | bytes 884744 | tf_op jit(solution)/shard_map/ppermute | solution.py:13
  177.2 14.2 %collective-permute-done.2 = f32[144,512]{1,0:T(8,128)S(1)} collective-permute-done((f32[144,512]{1,0:T(8,128)S(1)}, f32[144,512]{1,0:T(8,128)S(1)}, u32[]{:S(2)}, u32[]{:S(2)}) %collective-permute-start.2) | collective-permute-done | bytes 294944 | tf_op jit(solution)/shard_map/ppermute | solution.py:13
  191.4 0.8 add.64
  192.1 0.0 all-gather.9.cloned.1.call-update
  192.2 0.0 all-gather.11.cloned.1.call-start
  192.2 38.9 %all-gather.9.cloned.1.call-done = f32[576,512]{1,0:T(8,128)} async-done(((f32[144,512]{1,0:T(8,128)}), f32[576,512]{1,0:T(8,128)}) %all-gather.9.cloned.1.call-update) | async-done | bytes 1179664 | tf_op jit(solution)/shard_map/all_gather | solution.py:87
  231.1 0.0 all-gather.11.cloned.1.call-update
  231.1 22.1 %all-gather.11.cloned.1.call-done = f32[1152,512]{1,0:T(8,128)} async-done(((f32[576,512]{1,0:T(8,128)}), f32[1152,512]{1,0:T(8,128)}) %all-gather.11.cloned.1.call-update) | async-done | bytes 2359312 | tf_op jit(solution)/shard_map/all_gather | solution.py:88
  253.2 3.3 %copy.18 = f32[1,2,576,512]{3,2,1,0:T(8,128)} copy(f32[1,2,576,512]{3,2,1,0:T(8,128)} %bitcast.46) | data formatting | bytes 4718592
  (5 shorter events, 0.1 us)
Async XLA Ops:
  7.2 51.1 %copy-start = (bf16[1,1,128,512]{3,2,1,0:T(8,128)(2,1)S(1)}, bf16[1,1,128,512]{3,2,1,0:T(8,128)(2,1)}, u32[]{:S(2)}) copy-start(bf16[1,1,128,512]{3,2,1,0:T(8,128)(2,1)} %param.14) | copy-start | bytes 393220
  7.2 50.0 %all-gather.5.cloned.1.call-start = ((), (), s32[]{:S(2)}) async-start(), calls=%async_computation.2 | async-start | bytes 1638400 | tf_op jit(solution)/shard_map/all_gather | solution.py:74
  8.8 48.5 %copy-start.5 = (s32[1,1,128]{2,1,0:T(1,128)S(1)}, s32[1,1,128]{2,1,0:T(1,128)}, u32[]{:S(2)}) copy-start(s32[1,1,128]{2,1,0:T(1,128)} %param.13) | copy-start | bytes 1540
  11.5 46.7 %copy-start.3 = (f32[3,1,1,128]{3,2,1,0:T(1,128)S(1)}, f32[3,1,1,128]{3,2,1,0:T(1,128)}, u32[]{:S(2)}) copy-start(f32[3,1,1,128]{3,2,1,0:T(1,128)} %param.9) | copy-start | bytes 4612
  11.6 68.2 %all-gather.7.cloned.1.call-start = ((), (), s32[]{:S(2)}) async-start(), calls=%async_computation.3 | async-start | bytes 3932160 | tf_op jit(solution)/shard_map/all_gather | solution.py:75
  57.2 51.7 %reduce-scatter.3.cloned.1.call-start = ((), (), s32[]{:S(2)}) async-start(), calls=%async_computation.4 | async-start | bytes 3538944 | tf_op jit(solution)/shard_map/reduce_scatter | solution.py:84
  58.2 24.7 %copy-start.2 = (bf16[576,1,1,128]{3,0,2,1:T(8,128)(2,1)S(1)}, bf16[576,1,1,128]{3,0,2,1:T(8,128)(2,1)}, u32[]{:S(2)}) copy-start(bf16[576,1,1,128]{3,0,2,1:T(8,128)(2,1)} %param.12) | copy-start | bytes 442372
  58.2 24.7 %copy-start.4 = (f32[1,1,128]{2,1,0:T(1,128)S(1)}, f32[1,1,128]{2,1,0:T(1,128)}, u32[]{:S(2)}) copy-start(f32[1,1,128]{2,1,0:T(1,128)} %param.10) | copy-start | bytes 1540
  89.6 59.3 %copy-start.1 = (bf16[1,3,512,512]{3,2,1,0:T(8,128)(2,1)S(1)}, bf16[1,3,512,512]{3,2,1,0:T(8,128)(2,1)}, u32[]{:S(2)}) copy-start(bf16[1,3,512,512]{3,2,1,0:T(8,128)(2,1)} %param.15) | copy-start | bytes 4718596
  89.6 59.2 %reduce-scatter.5.cloned.1.call-start = ((), (), s32[]{:S(2)}) async-start(), calls=%async_computation.5 | async-start | bytes 1474560 | tf_op jit(solution)/shard_map/reduce_scatter | solution.py:85
  109.0 122.2 %all-gather.9.cloned.1.call-start = ((), (), s32[]{:S(2)}) async-start(), calls=%async_computation.6 | async-start | bytes 1474560 | tf_op jit(solution)/shard_map/all_gather | solution.py:87
  150.2 9.6 %collective-permute-start = (f32[144,512]{1,0:T(8,128)S(1)}, f32[144,512]{1,0:T(8,128)S(1)}, u32[]{:S(2)}, u32[]{:S(2)}) collective-permute-start(f32[144,512]{1,0:T(8,128)S(1)} %fusion.5), channel_id=1, source_target_pairs={{0,1},{1,0},{2,3},{3,2},{4,5},{5,4},{6,7},{7,6},{8,9},{9,8},{10,11... | collective-permute-start | bytes 884744 | tf_op jit(solution)/shard_map/ppermute | solution.py:13
  160.2 10.2 %collective-permute-start.1 = (f32[144,512]{1,0:T(8,128)S(1)}, f32[144,512]{1,0:T(8,128)S(1)}, u32[]{:S(2)}, u32[]{:S(2)}) collective-permute-start(f32[144,512]{1,0:T(8,128)S(1)} %fusion.3), channel_id=1, source_target_pairs={{0,2},{1,3},{2,0},{3,1},{4,6},{5,7},{6,4},{7,5},{8,10},{9,11},{10,... | collective-permute-start | bytes 884744 | tf_op jit(solution)/shard_map/ppermute | solution.py:13
  170.8 20.5 %collective-permute-start.2 = (f32[144,512]{1,0:T(8,128)S(1)}, f32[144,512]{1,0:T(8,128)S(1)}, u32[]{:S(2)}, u32[]{:S(2)}) collective-permute-start(f32[144,512]{1,0:T(8,128)S(1)} %fusion.1), channel_id=1, source_target_pairs={{0,4},{1,5},{2,6},{3,7},{4,0},{5,1},{6,2},{7,3},{8,12},{9,13},{10,... | collective-permute-start | bytes 884744 | tf_op jit(solution)/shard_map/ppermute | solution.py:13
  192.2 61.1 %all-gather.11.cloned.1.call-start = ((), (), s32[]{:S(2)}) async-start(), calls=%async_computation.7 | async-start | bytes 3538944 | tf_op jit(solution)/shard_map/all_gather | solution.py:88
Sparse Core Ops, SparseCore 0:
  11.7 45.4 all-gather.4
  59.3 20.4 all-gather.6
  89.8 19.1 reduce-scatter.2
  111.9 36.9 reduce-scatter.4
  192.3 38.7 all-gather.8
  233.3 19.9 all-gather.10
where the time goes:
time: 264 us; the launch traced here: 263 us
  waiting for transfers between devices  213 us (81%)
  between operations  14.3 us (5%)
  starting transfers between devices  14.2 us (5%)
  local copies, waits for them, and re-layouts  11 us (4%)
  matrix products  6.58 us (2%)
  other arithmetic  4.07 us (2%)
    all_gather x1, waiting for transfers between devices, shards(): piece = lax.all_gather(outgoing, 'ylo', axis=1, tiled=True)  45.6 us
    reduce_scatter x1, waiting for transfers between devices, shards(): mine = lax.psum_scatter(mine, 'ylo', scatter_dimension=0, tiled=True)  39.9 us
    all_gather x1, waiting for transfers between devices, shards(): top = lax.all_gather(top, 'ylo', axis=0, tiled=True)  38.9 us
    ppermute x3, waiting for transfers between devices, partner(): return lax.ppermute(value, axis, pairs)  26.3 us
    all_gather x1, waiting for transfers between devices, shards(): lax.all_gather(top, 'core', axis=0, tiled=True)  22.1 us
    all_gather x1, waiting for transfers between devices, shards(): piece = lax.all_gather(piece, 'core', axis=1, tiled=True)  21.1 us
    reduce_scatter x1, waiting for transfers between devices, shards(): mine = lax.psum_scatter(stacked, 'core', scatter_dimension=0, tiled=True)  19.3 us
    ppermute x3, starting transfers between devices, partner(): return lax.ppermute(value, axis, pairs)  14 us
  transfers between devices with their start and end apart: 9, of which 9 were waited for; matrix products, arithmetic and copies ran while one was open for 0% of the time, Pallas kernels for 0%

commit v1 on v0

--- a/solution.py
+++ b/solution.py
@@ -72,7 +72,10 @@
     )
     outgoing = jnp.concatenate([coords, area_row, scaled.astype(jnp.float32)], axis=0)
     piece = lax.all_gather(outgoing, "ylo", axis=1, tiled=True)
-    piece = lax.all_gather(piece, "core", axis=1, tiled=True)
+    near = jax.lax.axis_size("core")
+    part_next = jnp.stack(near * [piece])
+    e_next = jax.lax.all_to_all(part_next, "core", 0, 0)
+    piece = jnp.concatenate(e_next, axis=1)
     near_sum = near_block(coords, area_row[0], piece[:3], piece[3], piece[4:].astype(jnp.bfloat16))
     offdiag = (full_sketch.reshape(probe_count, panels).astype(jnp.float32) - near_sum).astype(
         jnp.bfloat16

time: 264 us -> 248 us (0.939)
  waiting for transfers between devices: 213 us -> 189 us
  blocking collectives: 0 us -> 7.4 us
    all_gather x1 -> x0, waiting for transfers between devices: 21.1 us -> none  [shards(): piece = lax.all_gather(piece, 'core', axis=1, tiled=True)]
    all_to_all x0 -> x1, blocking collectives: none -> 7.4 us  [shards(): e_next = jax.lax.all_to_all(part_next, 'core', 0, 0)]
    slice x1, local copies, waits for them, and re-layouts: 3.15 us -> 0.01 us  [kernel_tile(): gap = target_pos[component][:, None] - source_pos[component][None, :]]
    unnamed x15 -> x18, local copies, waits for them, and re-layouts: 5.16 us -> 6.3 us
  transfers between devices with their start and end apart: 9 -> 8, of which waited for: 9 -> 8; matrix products, arithmetic and copies ran while one was open for 0% -> 1% of each run, Pallas kernels for 0% -> 0%
where the time goes in v1:
time: 248 us; the launch traced here: 247 us
  waiting for transfers between devices  189 us (76%)
  starting transfers between devices  14.3 us (6%)
  between operations  14 us (6%)
  local copies, waits for them, and re-layouts  11.2 us (5%)
  blocking collectives  7.4 us (3%)
  other arithmetic  6.04 us (2%)
  matrix products  5.38 us (2%)
    all_gather x1, waiting for transfers between devices, shards(): piece = lax.all_gather(outgoing, 'ylo', axis=1, tiled=True)  43.2 us
    reduce_scatter x1, waiting for transfers between devices, shards(): mine = lax.psum_scatter(mine, 'ylo', scatter_dimension=0, tiled=True)  40 us
    all_gather x1, waiting for transfers between devices, shards(): top = lax.all_gather(top, 'ylo', axis=0, tiled=True)  39 us
    ppermute x3, waiting for transfers between devices, partner(): return lax.ppermute(value, axis, pairs)  26.1 us
    all_gather x1, waiting for transfers between devices, shards(): lax.all_gather(top, 'core', axis=0, tiled=True)  22.1 us
    reduce_scatter x1, waiting for transfers between devices, shards(): mine = lax.psum_scatter(stacked, 'core', scatter_dimension=0, tiled=True)  18.4 us
    ppermute x3, starting transfers between devices, partner(): return lax.ppermute(value, axis, pairs)  14.1 us
    all_to_all x1, blocking collectives, shards(): e_next = jax.lax.all_to_all(part_next, 'core', 0, 0)  7.4 us
  transfers between devices with their start and end apart: 8, of which 8 were waited for; matrix products, arithmetic and copies ran while one was open for 1% of the time, Pallas kernels for 0%

profile of v1, /device:TPU:1, one launch (start us, length us, event | category | flops | bytes accessed | tf_op | source)
XLA Modules:
  0.0 247.1 jit_solution(4932087240912312485)
XLA Ops:
  7.2 0.0 copy-start
  7.2 0.0 copy-start.6
  7.2 0.0 all-gather.4.cloned.1.call-start
  7.2 1.1 copy.23
  8.3 0.0 copy-start.4
  8.3 0.9 copy.22
  9.2 0.8 copy.24
  9.9 0.7 fusion.26
  10.7 0.9 pad_maximum_fusion.2
  11.6 0.0 all-gather.4.cloned.1.call-update
  11.6 0.0 reduce-scatter.3.cloned.1.call-start
  11.7 0.0 copy-done.6
  11.7 0.9 gather_fusion.1
  12.6 0.0 copy-done.4
  12.6 0.0 copy-done
  12.6 1.4 fusion.27
  14.1 43.2 %all-gather.4.cloned.1.call-done = f32[580,512]{0,1:T(8,128)} async-done(((f32[580,128]{0,1:T(8,128)}), f32[580,512]{0,1:T(8,128)}) %all-gather.4.cloned.1.call-update) | async-done | bytes 1187856 | tf_op jit(solution)/shard_map/all_gather | solution.py:74
  57.2 2.0 pad_maximum_fusion
  59.2 2.0 copy.25
  61.2 7.4 %all_to_all.5 = f32[2,580,512]{2,1,0:T(8,128)S(1)} all-to-all(f32[2,580,512]{2,1,0:T(8,128)} %copy.25), channel_id=1, replica_groups=mesh['ylo'=4,'core'=2,'leaf'=64] {'core'}, dimensions={0} | all-to-all | bytes 4751360 | tf_op jit(solution)/shard_map/all_to_all | solution.py:77
  68.7 0.3 fusion
  69.0 0.0 copy-start.3
  69.0 0.0 copy-start.5
  69.0 0.2 copy.28
  69.2 0.7 copy-done.3
  69.9 0.0 copy-done.5
  69.9 1.4 fusion.10
  71.3 0.0 copy-start.1
  71.3 0.2 copy.27
  71.5 0.9 gather_fusion
  72.4 0.4 fusion.29
  72.8 0.0 copy-done.1
  72.8 1.6 pad_maximum_fusion.1
  74.4 0.0 copy-start.2
  74.4 0.0 reduce-scatter.3.cloned.1.call-update
  74.5 0.0 reduce-scatter.5.cloned.1.call-start
  74.5 18.4 %reduce-scatter.3.cloned.1.call-done = f32[576,512]{1,0:T(8,128)} async-done(((f32[1152,512]{1,0:T(8,128)}), f32[576,512]{1,0:T(8,128)}) %reduce-scatter.3.cloned.1.call-update) | async-done | bytes 1179664 | tf_op jit(solution)/shard_map/reduce_scatter | solution.py:87
  92.9 0.0 reduce-scatter.5.cloned.1.call-update
  92.9 0.0 all-gather.6.cloned.1.call-start
  92.9 40.0 %reduce-scatter.5.cloned.1.call-done = f32[144,512]{1,0:T(8,128)} async-done(((f32[576,512]{1,0:T(8,128)}), f32[144,512]{1,0:T(8,128)}) %reduce-scatter.5.cloned.1.call-update) | async-done | bytes 294928 | tf_op jit(solution)/shard_map/reduce_scatter | solution.py:88
  132.9 0.0 copy-done.2
  132.9 1.4 fusion.5
  134.3 3.1 %collective-permute-start = (f32[144,512]{1,0:T(8,128)S(1)}, f32[144,512]{1,0:T(8,128)S(1)}, u32[]{:S(2)}, u32[]{:S(2)}) collective-permute-start(f32[144,512]{1,0:T(8,128)S(1)} %fusion.5), channel_id=1, source_target_pairs={{0,1},{1,0},{2,3},{3,2},{4,5},{5,4},{6,7},{7,6},{8,9},{9,8},{10,11... | collective-permute-start | bytes 884744 | tf_op jit(solution)/shard_map/ppermute | solution.py:13
  137.4 6.5 %collective-permute-done = f32[144,512]{1,0:T(8,128)S(1)} collective-permute-done((f32[144,512]{1,0:T(8,128)S(1)}, f32[144,512]{1,0:T(8,128)S(1)}, u32[]{:S(2)}, u32[]{:S(2)}) %collective-permute-start) | collective-permute-done | bytes 294944 | tf_op jit(solution)/shard_map/ppermute | solution.py:13
  143.9 0.4 fusion.3
  144.3 4.6 %collective-permute-start.1 = (f32[144,512]{1,0:T(8,128)S(1)}, f32[144,512]{1,0:T(8,128)S(1)}, u32[]{:S(2)}, u32[]{:S(2)}) collective-permute-start(f32[144,512]{1,0:T(8,128)S(1)} %fusion.3), channel_id=1, source_target_pairs={{0,2},{1,3},{2,0},{3,1},{4,6},{5,7},{6,4},{7,5},{8,10},{9,11},{10,... | collective-permute-start | bytes 884744 | tf_op jit(solution)/shard_map/ppermute | solution.py:13
  148.9 5.5 %collective-permute-done.1 = f32[144,512]{1,0:T(8,128)S(1)} collective-permute-done((f32[144,512]{1,0:T(8,128)S(1)}, f32[144,512]{1,0:T(8,128)S(1)}, u32[]{:S(2)}, u32[]{:S(2)}) %collective-permute-start.1) | collective-permute-done | bytes 294944 | tf_op jit(solution)/shard_map/ppermute | solution.py:13
  154.4 0.4 fusion.1
  154.8 6.4 %collective-permute-start.2 = (f32[144,512]{1,0:T(8,128)S(1)}, f32[144,512]{1,0:T(8,128)S(1)}, u32[]{:S(2)}, u32[]{:S(2)}) collective-permute-start(f32[144,512]{1,0:T(8,128)S(1)} %fusion.1), channel_id=1, source_target_pairs={{0,4},{1,5},{2,6},{3,7},{4,0},{5,1},{6,2},{7,3},{8,12},{9,13},{10,... | collective-permute-start | bytes 884744 | tf_op jit(solution)/shard_map/ppermute | solution.py:13
  161.2 14.1 %collective-permute-done.2 = f32[144,512]{1,0:T(8,128)S(1)} collective-permute-done((f32[144,512]{1,0:T(8,128)S(1)}, f32[144,512]{1,0:T(8,128)S(1)}, u32[]{:S(2)}, u32[]{:S(2)}) %collective-permute-start.2) | collective-permute-done | bytes 294944 | tf_op jit(solution)/shard_map/ppermute | solution.py:13
  175.3 0.8 add.64
  176.1 0.0 all-gather.6.cloned.1.call-update
  176.1 0.0 all-gather.8.cloned.1.call-start
  176.2 39.0 %all-gather.6.cloned.1.call-done = f32[576,512]{1,0:T(8,128)} async-done(((f32[144,512]{1,0:T(8,128)}), f32[576,512]{1,0:T(8,128)}) %all-gather.6.cloned.1.call-update) | async-done | bytes 1179664 | tf_op jit(solution)/shard_map/all_gather | solution.py:90
  215.2 0.0 all-gather.8.cloned.1.call-update
  215.2 22.1 %all-gather.8.cloned.1.call-done = f32[1152,512]{1,0:T(8,128)} async-done(((f32[576,512]{1,0:T(8,128)}), f32[1152,512]{1,0:T(8,128)}) %all-gather.8.cloned.1.call-update) | async-done | bytes 2359312 | tf_op jit(solution)/shard_map/all_gather | solution.py:91
  237.3 3.3 %copy.30 = f32[1,2,576,512]{3,2,1,0:T(8,128)} copy(f32[1,2,576,512]{3,2,1,0:T(8,128)} %bitcast.58) | data formatting | bytes 4718592
  (6 shorter events, 0.1 us)
Async XLA Ops:
  7.2 5.5 %copy-start = (bf16[1,1,128,512]{3,2,1,0:T(8,128)(2,1)S(1)}, bf16[1,1,128,512]{3,2,1,0:T(8,128)(2,1)}, u32[]{:S(2)}) copy-start(bf16[1,1,128,512]{3,2,1,0:T(8,128)(2,1)} %param.14) | copy-start | bytes 393220
  7.2 4.5 %copy-start.6 = (s32[1,1,128]{2,1,0:T(1,128)S(1)}, s32[1,1,128]{2,1,0:T(1,128)}, u32[]{:S(2)}) copy-start(s32[1,1,128]{2,1,0:T(1,128)} %param.13) | copy-start | bytes 1540
  7.2 50.1 %all-gather.4.cloned.1.call-start = ((), (), s32[]{:S(2)}) async-start(), calls=%async_computation.3 | async-start | bytes 1638400 | tf_op jit(solution)/shard_map/all_gather | solution.py:74
  8.3 4.3 %copy-start.4 = (f32[3,1,1,128]{3,2,1,0:T(1,128)S(1)}, f32[3,1,1,128]{3,2,1,0:T(1,128)}, u32[]{:S(2)}) copy-start(f32[3,1,1,128]{3,2,1,0:T(1,128)} %param.9) | copy-start | bytes 4612
  11.6 81.2 %reduce-scatter.3.cloned.1.call-start = ((), (), s32[]{:S(2)}) async-start(), calls=%async_computation.4 | async-start | bytes 3538944 | tf_op jit(solution)/shard_map/reduce_scatter | solution.py:87
  69.0 0.9 copy-start.3
  69.0 0.9 copy-start.5
  71.3 1.5 copy-start.1
  74.4 58.5 %copy-start.2 = (bf16[1,3,512,512]{3,2,1,0:T(8,128)(2,1)S(1)}, bf16[1,3,512,512]{3,2,1,0:T(8,128)(2,1)}, u32[]{:S(2)}) copy-start(bf16[1,3,512,512]{3,2,1,0:T(8,128)(2,1)} %param.15) | copy-start | bytes 4718596
  74.5 58.5 %reduce-scatter.5.cloned.1.call-start = ((), (), s32[]{:S(2)}) async-start(), calls=%async_computation.5 | async-start | bytes 1474560 | tf_op jit(solution)/shard_map/reduce_scatter | solution.py:88
  92.9 122.3 %all-gather.6.cloned.1.call-start = ((), (), s32[]{:S(2)}) async-start(), calls=%async_computation.6 | async-start | bytes 1474560 | tf_op jit(solution)/shard_map/all_gather | solution.py:90
  134.3 9.6 %collective-permute-start = (f32[144,512]{1,0:T(8,128)S(1)}, f32[144,512]{1,0:T(8,128)S(1)}, u32[]{:S(2)}, u32[]{:S(2)}) collective-permute-start(f32[144,512]{1,0:T(8,128)S(1)} %fusion.5), channel_id=1, source_target_pairs={{0,1},{1,0},{2,3},{3,2},{4,5},{5,4},{6,7},{7,6},{8,9},{9,8},{10,11... | collective-permute-start | bytes 884744 | tf_op jit(solution)/shard_map/ppermute | solution.py:13
  144.3 10.2 %collective-permute-start.1 = (f32[144,512]{1,0:T(8,128)S(1)}, f32[144,512]{1,0:T(8,128)S(1)}, u32[]{:S(2)}, u32[]{:S(2)}) collective-permute-start(f32[144,512]{1,0:T(8,128)S(1)} %fusion.3), channel_id=1, source_target_pairs={{0,2},{1,3},{2,0},{3,1},{4,6},{5,7},{6,4},{7,5},{8,10},{9,11},{10,... | collective-permute-start | bytes 884744 | tf_op jit(solution)/shard_map/ppermute | solution.py:13
  154.8 20.5 %collective-permute-start.2 = (f32[144,512]{1,0:T(8,128)S(1)}, f32[144,512]{1,0:T(8,128)S(1)}, u32[]{:S(2)}, u32[]{:S(2)}) collective-permute-start(f32[144,512]{1,0:T(8,128)S(1)} %fusion.1), channel_id=1, source_target_pairs={{0,4},{1,5},{2,6},{3,7},{4,0},{5,1},{6,2},{7,3},{8,12},{9,13},{10,... | collective-permute-start | bytes 884744 | tf_op jit(solution)/shard_map/ppermute | solution.py:13
  176.1 61.2 %all-gather.8.cloned.1.call-start = ((), (), s32[]{:S(2)}) async-start(), calls=%async_computation.7 | async-start | bytes 3538944 | tf_op jit(solution)/shard_map/all_gather | solution.py:91
Sparse Core Ops, SparseCore 0:
  11.7 45.4 all-gather.3
  74.6 18.2 reduce-scatter.2
  96.0 36.8 reduce-scatter.4
  176.2 38.8 all-gather.5
  217.3 19.9 all-gather.7
